TPU v7x, 32 devices: a whole 2x2x4 slice. The times are simulated.
32 devices in a mesh: scene: 2 (over y), bins: 4 (over z), az: 4 (over x, core).
Axes of the slice: x: 2, y: 2, z: 4, core: 2. Of those that a mesh axis runs over, the one named last changes fastest.
Arguments:
- raw_echoes: bfloat16 [2, 8, 512, 16384], P(None, ('scene', 'az'), 'bins'), parts along dimension 1, may hold values from -6 to 6
- range_phase: float32 [16384], replicated, may hold values from -3.140625 to 3.140625
- band_start: int32 [16384], replicated, may hold values from 0 to 16447, as said below
- band_weight: bfloat16 [8, 16384], replicated, may hold values from -0.25 to 0.75
- intersection_length: int32 [16384], P('bins'), may hold values from 32 to 128
- azimuth_rate: float32 [16384], P('bins'), may hold values from 0.25 to 2
Outputs:
- focused_image: bfloat16 [2, 8, 512, 16384], P(None, ('scene', 'az'), None, 'bins'), parts along dimension 1
There are 2 independent parts, one for each index of `scene`. A program takes and returns all parts, laid end to end along the dimension named above; an argument that names none is the same for every part. Nothing has to cross between parts.
Inputs may be any that keep to these rules, and one draw needn't show every extreme that they name: band_start[b] - b lies between 0 and 64 for every range bin b.
All inputs are finite; a program needn't handle non-finite values.
Results may differ from a plain program's by a relative error of at most 0.02.
Values may be sent and summed in bfloat16 or wider, within the bound.
A program may use at most 128 MiB of HBM per device.

v0:
```python
import math
import jax
import jax.numpy as jnp
from jax import lax
from jax.sharding import PartitionSpec as P

OVLMAX = 128


def passed_along(value, axis, steps):
    count = lax.axis_size(axis)
    first, last = (max(0, -steps), min(count, count - steps))
    return lax.ppermute(value, axis, [(source, source + steps) for source in range(first, last)])


def phase_pair(row_count, col_count, length, direction):
    row_index = jnp.arange(row_count, dtype=jnp.int32)[:, None]
    col_index = jnp.arange(col_count, dtype=jnp.int32)[None, :]
    product = (row_index * col_index % length).astype(jnp.float32)
    phase_angle = product * (direction * 2.0 * math.pi / length)
    return (jnp.cos(phase_angle), jnp.sin(phase_angle))


def narrow_pair(operands):
    return (operands[0].astype(jnp.bfloat16), operands[1].astype(jnp.bfloat16))


def complex_product(form, left_pair, right_pair):
    left_real, left_imag = left_pair
    right_real, right_imag = right_pair
    real_part = jnp.einsum(
        form, left_real, right_real, preferred_element_type=jnp.float32
    ) - jnp.einsum(form, left_imag, right_imag, preferred_element_type=jnp.float32)
    imag_part = jnp.einsum(
        form, left_real, right_imag, preferred_element_type=jnp.float32
    ) + jnp.einsum(form, left_imag, right_real, preferred_element_type=jnp.float32)
    return (real_part, imag_part)


def complex_scale(operands, cosine, sine_part):
    real_part = operands[0] * cosine - operands[1] * sine_part
    imag_part = operands[0] * sine_part + operands[1] * cosine
    return (real_part, imag_part)


def compress_lines(echo_lines, range_phase):
    line_count, line_width = (echo_lines.shape[1], echo_lines.shape[2])
    radix_size = 128
    other_size = line_width // radix_size
    line_grid = echo_lines.reshape(2, line_count, radix_size, other_size)
    first_table = narrow_pair(phase_pair(radix_size, radix_size, radix_size, -1.0))
    partial_value = complex_product("ka,pan->pkn", first_table, (line_grid[0], line_grid[1]))
    partial_value = complex_scale(
        partial_value, *phase_pair(radix_size, other_size, line_width, -1.0)
    )
    second_table = narrow_pair(phase_pair(other_size, other_size, other_size, -1.0))
    spectrum = complex_product("pkn,nm->pkm", narrow_pair(partial_value), second_table)
    filter_angle = range_phase.reshape(other_size, radix_size).T
    filtered = narrow_pair(complex_scale(spectrum, jnp.cos(filter_angle), -jnp.sin(filter_angle)))
    back_table = narrow_pair(phase_pair(other_size, other_size, other_size, 1.0))
    partial_value = complex_product("pkm,mn->pkn", filtered, back_table)
    partial_value = complex_scale(
        partial_value, *phase_pair(radix_size, other_size, line_width, 1.0)
    )
    last_table = narrow_pair(phase_pair(radix_size, radix_size, radix_size, 1.0))
    result = complex_product("ak,pkn->pan", last_table, narrow_pair(partial_value))
    stacked = jnp.stack(result) * (1.0 / line_width)
    return stacked.reshape(2, line_count, line_width).astype(jnp.bfloat16)


def migrate(samples, range_rim, starts, weights):
    row_count, line_width = (samples.shape[1], samples.shape[2])
    blocks = line_width // 128
    extended = jnp.concatenate([samples, range_rim], axis=2)
    windows = jnp.concatenate(
        [
            extended[:, :, :line_width].reshape(2, row_count, blocks, 128),
            extended[:, :, 128:].reshape(2, row_count, blocks, 128),
        ],
        axis=3,
    )
    block_start = 128 * jnp.arange(blocks, dtype=jnp.int32)[:, None]
    offsets = starts.reshape(blocks, 128) - block_start
    position = jnp.arange(256, dtype=jnp.int32)[None, :, None]
    band_matrix = jnp.zeros((blocks, 256, 128), jnp.bfloat16)
    for tap_index in range(weights.shape[0]):
        tap_weight = weights[tap_index].reshape(blocks, 128)[:, None, :]
        band_matrix = band_matrix + jnp.where(
            position == (offsets + tap_index)[:, None, :], tap_weight, jnp.zeros((), jnp.bfloat16)
        )
    result = jnp.einsum("sprj,rjk->sprk", windows, band_matrix, preferred_element_type=jnp.float32)
    return result.reshape(2, row_count, line_width).astype(jnp.bfloat16)


def shards(raw_echoes, range_phase, band_start, band_weight, intersection_length, azimuth_rate):
    echo_lines = raw_echoes[:, 0]
    compressed = compress_lines(echo_lines, range_phase)
    empty_rim = jnp.zeros((2, compressed.shape[1], 128), jnp.bfloat16)
    outgoing = migrate(compressed, empty_rim, band_start, band_weight)
    turned = lax.all_to_all(outgoing, "bins", split_axis=2, concat_axis=1, tiled=True)
    head_lines = passed_along(turned[:, :OVLMAX], "az", -1)
    aperture = jnp.concatenate([turned, head_lines], axis=1)
    own_count = turned.shape[1]
    length = aperture.shape[1]
    pulses = jnp.arange(length, dtype=jnp.int32)[:, None]
    inside = (pulses < own_count) | (pulses - own_count < intersection_length[None, :])
    aperture = jnp.where(inside[None], aperture, jnp.zeros((), jnp.bfloat16))
    forward_table = narrow_pair(phase_pair(length, length, length, -1.0))
    spectrum = complex_product("fp,pr->fr", forward_table, (aperture[0], aperture[1]))
    doppler = jnp.arange(length, dtype=jnp.int32)
    signed = jnp.where(2 * doppler >= length, doppler - length, doppler).astype(jnp.float32)
    phase_angle = math.pi * azimuth_rate[None, :] * (signed * signed)[:, None] / length
    focused = narrow_pair(complex_scale(spectrum, jnp.cos(phase_angle), -jnp.sin(phase_angle)))
    inverse_table = narrow_pair(phase_pair(own_count, length, length, 1.0))
    image_pair = complex_product("qf,fr->qr", inverse_table, focused)
    stacked = jnp.stack(image_pair) * (1.0 / length)
    return stacked.astype(jnp.bfloat16)[:, None]


def solution(mesh):
    in_specs = (P(None, ("scene", "az"), "bins", None), P(), P(), P(), P("bins"), P("bins"))
    out_specs = P(None, ("scene", "az"), None, "bins")
    return jax.shard_map(shards, mesh=mesh, in_specs=in_specs, out_specs=out_specs, check_vma=False)
```

profile of v0, /device:TPU:1, one launch (start us, length us, event | category | flops | bytes accessed | tf_op | source)
XLA Modules:
  0.0 641.5 jit_solution(2054546862084710419)
XLA Ops:
  0.0 3.9 slice_bitcast_fusion.7
  5.1 4.9 fusion.105
  10.0 4.7 fusion.99
  16.2 4.7 fusion.97
  20.9 10.6 %fusion.42 = (bf16[128,128,128]{2,1,0:T(8,128)(2,1)S(1)}, bf16[128,128,128]{2,1,0:T(8,128)(2,1)S(1)}) fusion(f32[128,128]{1,0:T(8,128)S(1)} %get-tuple-element.37, f32[128,128]{1,0:T(8,128)S(1)} %get-tuple-element.38, f32[128,128,128]{2,0,1:T(8,128)} %fusion.105, f32[128,128,128]{2,0,1:T(8,128)} %fusion.97, f32[128,128,128]{2,0,1:T(8,128)} %fusion.99, ...), kind=kOutput, calls=%fused_computation.64 | convolution fusion | flops 558088192 | bytes 37879808 | tf_op jit(solution)/shard_map/ka,pan->pkn/dot_general | solution.py:31
  31.5 4.9 fusion.101
  36.4 4.7 fusion.95
  41.1 4.7 fusion.103
  46.2 13.0 %add_convert_fusion.2 = (bf16[128,128,128]{2,1,0:T(8,128)(2,1)S(1)}, bf16[128,128,128]{2,1,0:T(8,128)(2,1)S(1)}) fusion(f32[128,128]{1,0:T(8,128)S(1)} %copy.36, f32[128,128]{1,0:T(8,128)S(1)} %copy.35, f32[128,128,128]{2,1,0:T(8,128)} %fusion.101, f32[128,128,128]{2,1,0:T(8,128)} %fusion.103, f32[128,128,128]{2,1,0:T(8,128)} %fusion.95, ...), kind=kOutput, calls=%fused_computation.45 | convolution fusion | flops 558088192 | bytes 37879808 | tf_op jit(solution)/shard_map/pkn,nm->pkm/dot_general | solution.py:34
  59.2 4.7 fusion.83
  63.9 4.9 fusion.89
  69.1 4.7 fusion.91
  73.8 12.9 %subtract_convert_fusion.1 = (bf16[128,128,128]{2,1,0:T(8,128)(2,1)}, bf16[128,128,128]{2,1,0:T(8,128)(2,1)S(1)}) fusion(f32[128,128]{1,0:T(8,128)S(1)} %get-tuple-element.39, f32[128,128]{1,0:T(8,128)S(1)} %get-tuple-element.40, f32[128,128,128]{2,1,0:T(8,128)} %fusion.89, f32[128,128,128]{2,1,0:T(8,128)} %fusion.91, f32[128,128,128]{2,1,0:T(8,128)} %fusion.83, ...), kind=kOutput, calls=%fused_computation.44 | convolution fusion | flops 558088192 | bytes 37879808 | tf_op jit(solution)/shard_map/pkm,mn->pkn/dot_general | solution.py:34
  86.7 4.9 fusion.79
  91.6 1.5 fusion.77
  93.1 10.6 %subtract_bitcast_fusion.1 = (f32[1,128,128,128]{2,3,1,0:T(8,128)}, f32[128,128,128]{1,2,0:T(8,128)}) fusion(f32[128,128,128]{2,1,0:T(8,128)} %fusion.79, bf16[128,128,128]{2,1,0:T(8,128)(2,1)S(1)} %copy-done.1), kind=kOutput, calls=%fused_computation.78 | convolution fusion | flops 539213824 | bytes 29360128 | tf_op jit(solution)/shard_map/ak,pkn->pan/dot_general | solution.py:31
  103.7 7.5 %add_bitcast_fusion.1 = (f32[1,128,128,128]{2,3,1,0:T(8,128)}, f32[128,128,128]{1,2,0:T(8,128)}) fusion(f32[128,128,128]{2,1,0:T(8,128)S(1)} %fusion.77, bf16[128,128,128]{2,1,0:T(8,128)(2,1)S(1)} %get-tuple-element.16), kind=kOutput, calls=%fused_computation.76 | convolution fusion | flops 539213824 | bytes 29360128 | tf_op jit(solution)/shard_map/ak,pkn->pan/dot_general | solution.py:34
  111.2 9.4 %copy.41 = f32[128,128,128]{0,2,1:T(8,128)} copy(f32[128,128,128]{1,2,0:T(8,128)} %get-tuple-element.24) | data formatting | bytes 16777216 | tf_op jit(solution)/shard_map/sub | solution.py:31
  120.6 9.4 %copy.42 = f32[128,128,128]{0,2,1:T(8,128)} copy(f32[128,128,128]{1,2,0:T(8,128)} %get-tuple-element.26) | data formatting | bytes 16777216 | tf_op jit(solution)/shard_map/add | solution.py:34
  130.1 6.7 %fusion.1 = bf16[2,128,16384]{1,2,0:T(8,128)(2,1)S(1)} fusion(f32[1,128,16384]{1,2,0:T(8,128)} %bitcast.146, f32[1,128,16384]{1,2,0:T(8,128)} %bitcast.145), kind=kLoop, calls=%fused_computation.3 | loop fusion | flops 12582912 | bytes 25165824 | tf_op jit(solution)/shard_map/convert_element_type | solution.py:68
  136.7 3.7 pad_slice_fusion
  140.4 13.6 %copy.43 = bf16[2,128,128,128]{2,3,1,0:T(8,128)(2,1)} copy(bf16[2,128,128,128]{1,3,2,0:T(8,128)(2,1)} %bitcast.147) | data formatting | bytes 16777216 | tf_op jit(solution)/shard_map/reshape | solution.py:78
  154.0 7.1 %fusion = bf16[2,128,128,128]{2,3,1,0:T(8,128)(2,1)S(1)} fusion(f32[1,128,128,128]{2,3,1,0:T(8,128)} %get-tuple-element.25, f32[1,128,128,128]{2,3,1,0:T(8,128)} %get-tuple-element.23), kind=kLoop, calls=%fused_computation.1 | loop fusion | flops 12582912 | bytes 25165824 | tf_op jit(solution)/shard_map/convert_element_type | solution.py:68
  162.2 6.5 %pad_maximum_fusion = bf16[2,128,128,256]{2,3,1,0:T(8,128)(2,1)} fusion(bf16[2,128,128,128]{2,3,1,0:T(8,128)(2,1)S(1)} %copy-done.2, bf16[2,128,128,128]{2,3,1,0:T(8,128)(2,1)S(1)} %fusion), kind=kLoop, calls=%fused_computation.4 | loop fusion | flops 33554432 | bytes 33554432 | tf_op jit(solution)/shard_map/concatenate | solution.py:75
  168.7 23.6 %copy.44 = bf16[2,128,128,256]{3,1,0,2:T(8,128)(2,1)} copy(bf16[2,128,128,256]{2,3,1,0:T(8,128)(2,1)} %pad_maximum_fusion) | data formatting | bytes 33554432 | tf_op jit(solution)/shard_map/concatenate | solution.py:75
  192.5 1.4 slice_reduce_fusion.7
  193.9 38.2 %fusion.232 = bf16[128,256,128,1]{1,2,3,0:T(8,128)(2,1)} fusion(s32[128,128]{1,0:T(8,128)S(1)} %get-tuple-element.34, s32[128,128]{1,0:T(8,128)S(1)} %get-tuple-element.30, s32[128,128]{1,0:T(8,128)S(1)} %get-tuple-element.31, s32[128,128]{1,0:T(8,128)S(1)} %get-tuple-element.32, s32[128,128]{1,0:T(8,128)S(1)} %get-tuple-element.33, ...), kind=kLoop, calls=%fused_computation.32.clone.clone.clone.clone.1 | loop fusion | flops 134217728 | bytes 9175040 | tf_op jit(solution)/shard_map/sprj,rjk->sprk/dot_general | solution.py:91
  232.1 13.1 %convert_bitcast_fusion = bf16[2,128,128,128]{1,3,0,2:T(8,128)(2,1)} fusion(bf16[2,128,128,256]{3,1,0,2:T(8,128)(2,1)} %copy.44, bf16[128,256,128,1]{1,2,3,0:T(8,128)(2,1)} %fusion.232), kind=kOutput, calls=%fused_computation.42 | convolution fusion | flops 2151677952 | bytes 33554432 | tf_op jit(solution)/shard_map/sprj,rjk->sprk/dot_general | solution.py:91
  245.2 10.5 %copy.45 = bf16[2,128,128,128]{1,3,2,0:T(8,128)(2,1)} copy(bf16[2,128,128,128]{1,3,0,2:T(8,128)(2,1)} %convert_bitcast_fusion) | data formatting | bytes 16777216 | tf_op jit(solution)/shard_map/convert_element_type | solution.py:92
  255.7 15.6 %copy.46 = bf16[2,128,16384]{1,0,2:T(2,128)(2,1)S(1)} copy(bf16[2,128,16384]{1,2,0:T(8,128)(2,1)} %bitcast.148) | data formatting | bytes 16777216 | tf_op jit(solution)/shard_map/convert_element_type | solution.py:92
  271.3 187.4 %all_to_all.18 = bf16[2,128,16384]{1,0,2:T(2,128)(2,1)S(1)} all-to-all(bf16[2,128,16384]{1,0,2:T(2,128)(2,1)S(1)} %copy.46), channel_id=1, replica_groups=mesh['scene'=2,'bins'=4,'az'=4] {'bins'}, dimensions={2} | all-to-all | bytes 16777216 | tf_op jit(solution)/shard_map/all_to_all | solution.py:100
  458.7 10.5 %copy.47 = bf16[2,128,16384]{1,2,0:T(8,128)(2,1)} copy(bf16[2,128,16384]{1,0,2:T(2,128)(2,1)S(1)} %all_to_all.18) | data formatting | bytes 16777216 | tf_op jit(solution)/shard_map/all_to_all | solution.py:100
  469.3 12.1 %copy.48 = bf16[2,4,128,4096]{3,2,1,0:T(8,128)(2,1)} copy(bf16[2,4,128,4096]{2,3,1,0:T(8,128)(2,1)} %bitcast.149) | data formatting | bytes 16777216 | tf_op jit(solution)/shard_map/all_to_all | solution.py:100
  481.4 1.7 slice.58
  483.1 3.7 collective-permute-start
  486.8 6.5 %cosine_convert_fusion.2.clone.5 = bf16[640,640]{1,0:T(8,128)(2,1)S(1)} fusion(), kind=kLoop, calls=%fused_computation.85.clone.clone.clone.clone.2 | loop fusion | flops 4096000 | bytes 819200 | tf_op jit(solution)/shard_map/convert_element_type | solution.py:25
  493.4 2.3 compare_or_fusion
  495.7 15.8 %collective-permute-done = bf16[2,128,4096]{2,1,0:T(8,128)(2,1)S(1)} collective-permute-done((bf16[2,128,4096]{2,1,0:T(8,128)(2,1)S(1)}, bf16[2,128,4096]{2,1,0:T(8,128)(2,1)S(1)}, u32[]{:S(2)}, u32[]{:S(2)}) %collective-permute-start) | collective-permute-done | bytes 2097184 | tf_op jit(solution)/shard_map/ppermute | solution.py:13
  511.6 7.9 %maximum_select_fusion = bf16[2,640,4096]{2,1,0:T(8,128)(2,1)S(1)} fusion(bf16[2,128,4096]{2,1,0:T(8,128)(2,1)S(1)} %collective-permute-done, bf16[2,512,4096]{2,1,0:T(8,128)(2,1)} %bitcast.140, pred[640,4096]{1,0:T(8,128)(4,1)S(1)} %compare_or_fusion), kind=kLoop, calls=%fused_computation.23 | loop fusion | flops 26214400 | bytes 23592960 | tf_op jit(solution)/shard_map/jit(_where)/select_n | solution.py:107
  519.5 12.6 %fusion.40 = f32[640,4096]{1,0:T(8,128)} fusion(bf16[2,640,4096]{2,1,0:T(8,128)(2,1)S(1)} %maximum_select_fusion), kind=kOutput, calls=%fused_computation.62 | convolution fusion | flops 3359539200 | bytes 15728640 | tf_op jit(solution)/shard_map/fp,pr->fr/dot_general | solution.py:33
  532.1 12.9 %fusion.39 = f32[640,4096]{1,0:T(8,128)} fusion(bf16[2,640,4096]{2,1,0:T(8,128)(2,1)S(1)} %maximum_select_fusion), kind=kOutput, calls=%fused_computation.61 | convolution fusion | flops 3359539200 | bytes 15728640 | tf_op jit(solution)/shard_map/fp,pr->fr/dot_general | solution.py:36
  545.0 12.9 %convolution_subtract_fusion = f32[640,4096]{1,0:T(8,128)S(1)} fusion(f32[640,4096]{1,0:T(8,128)} %fusion.40, bf16[2,640,4096]{2,1,0:T(8,128)(2,1)S(1)} %maximum_select_fusion), kind=kOutput, calls=%fused_computation.58 | convolution fusion | flops 3362160640 | bytes 26214400 | tf_op jit(solution)/shard_map/fp,pr->fr/dot_general | solution.py:31
  557.9 46.4 %subtract_convert_fusion = (bf16[640,4096]{1,0:T(8,128)(2,1)S(1)}, bf16[640,4096]{1,0:T(8,128)(2,1)}) fusion(f32[640,4096]{1,0:T(8,128)S(1)} %convolution_subtract_fusion, f32[640]{0:T(1024)S(1)} %fusion.111, f32[4096]{0:T(1024)S(1)} %broadcast_multiply_fusion, f32[640,4096]{1,0:T(8,128)} %fusion.39, bf16[2,640,4096]{2,1,0:T(8,128)(2,1)S(1)} %maximum_select_fusion, ...), kind=kOutput, calls=%fused_computation.25 | convolution fusion | flops 3386900480 | bytes 37539840 | tf_op jit(solution)/shard_map/fp,pr->fr/dot_general | solution.py:34
  604.4 8.0 %fusion.63 = f32[512,4096]{1,0:T(8,128)S(1)} fusion(bf16[640,4096]{1,0:T(8,128)(2,1)S(1)} %get-tuple-element.21), kind=kOutput, calls=%fused_computation.99 | convolution fusion | flops 2687631360 | bytes 13631488 | tf_op jit(solution)/shard_map/qf,fr->qr/dot_general | solution.py:31
  612.4 8.4 %fusion.62 = f32[512,4096]{1,0:T(8,128)S(1)} fusion(bf16[640,4096]{1,0:T(8,128)(2,1)S(1)} %bitcast.159), kind=kOutput, calls=%fused_computation.98 | convolution fusion | flops 2687631360 | bytes 13631488 | tf_op jit(solution)/shard_map/qf,fr->qr/dot_general | solution.py:34
  620.9 8.1 %subtract_bitcast_fusion = f32[1,1,512,4096]{3,2,1,0:T(8,128)S(1)} fusion(f32[512,4096]{1,0:T(8,128)S(1)} %fusion.63, bf16[640,4096]{1,0:T(8,128)(2,1)S(1)} %bitcast.159), kind=kOutput, calls=%fused_computation.41 | convolution fusion | flops 2689728512 | bytes 22020096 | tf_op jit(solution)/shard_map/qf,fr->qr/dot_general | solution.py:33
  629.0 8.3 %add_bitcast_fusion = f32[1,1,512,4096]{3,2,1,0:T(8,128)S(1)} fusion(f32[512,4096]{1,0:T(8,128)S(1)} %fusion.62, bf16[640,4096]{1,0:T(8,128)(2,1)S(1)} %copy-done.9), kind=kOutput, calls=%fused_computation.40 | convolution fusion | flops 2689728512 | bytes 22020096 | tf_op jit(solution)/shard_map/qf,fr->qr/dot_general | solution.py:36
  637.2 4.1 fusion.2
  (39 shorter events, 4.7 us)
Async XLA Ops:
  31.5 9.6 %copy-start = (bf16[128,128,128]{2,1,0:T(8,128)(2,1)}, bf16[128,128,128]{2,1,0:T(8,128)(2,1)S(1)}, u32[]{:S(2)}) copy-start(bf16[128,128,128]{2,1,0:T(8,128)(2,1)S(1)} %get-tuple-element.20) | copy-start | bytes 12582916
  41.1 4.7 copy-start.4
  86.7 4.9 copy-start.1
  154.0 8.2 %copy-start.2 = (bf16[2,128,128,128]{2,3,1,0:T(8,128)(2,1)S(1)}, bf16[2,128,128,128]{2,3,1,0:T(8,128)(2,1)}, u32[]{:S(2)}) copy-start(bf16[2,128,128,128]{2,3,1,0:T(8,128)(2,1)} %copy.43) | copy-start | bytes 25165828
  168.7 23.7 %copy-start.5 = (s32[16384]{0:T(1024)S(1)}, s32[16384]{0:T(1024)}, u32[]{:S(2)}) copy-start(s32[16384]{0:T(1024)} %param.8) | copy-start | bytes 196612
  168.7 23.8 %copy-start.3 = (bf16[8,16384]{1,0:T(8,128)(2,1)S(1)}, bf16[8,16384]{1,0:T(8,128)(2,1)}, u32[]{:S(2)}) copy-start(bf16[8,16384]{1,0:T(8,128)(2,1)} %param.9) | copy-start | bytes 786436
  469.3 24.1 %copy-start.7 = (f32[4096]{0:T(1024)S(1)}, f32[4096]{0:T(1024)}, u32[]{:S(2)}) copy-start(f32[4096]{0:T(1024)} %param.11) | copy-start | bytes 49156
  469.3 24.1 %copy-start.6 = (s32[4096]{0:T(1024)S(1)}, s32[4096]{0:T(1024)}, u32[]{:S(2)}) copy-start(s32[4096]{0:T(1024)} %param.10) | copy-start | bytes 49156
  483.1 28.5 %collective-permute-start = (bf16[2,128,4096]{2,1,0:T(8,128)(2,1)S(1)}, bf16[2,128,4096]{2,1,0:T(8,128)(2,1)S(1)}, u32[]{:S(2)}, u32[]{:S(2)}) collective-permute-start(bf16[2,128,4096]{2,1,0:T(8,128)(2,1)S(1)} %slice.58), channel_id=1, source_target_pairs={{1,0},{2,1},{3,2},{5,4},{6,5},{7,6},{9,8},{10,9},{11,10},{13,12},{... | collective-permute-start | bytes 6291464 | tf_op jit(solution)/shard_map/ppermute | solution.py:13
  604.3 8.1 %copy-start.8 = (bf16[640,4096]{1,0:T(8,128)(2,1)}, bf16[640,4096]{1,0:T(8,128)(2,1)S(1)}, u32[]{:S(2)}) copy-start(bf16[640,4096]{1,0:T(8,128)(2,1)S(1)} %get-tuple-element.21) | copy-start | bytes 15728644
  604.3 8.1 %slice-start = ((s8[5242880]{0:T(1024)(128)(4,1)}), s8[4194304]{0:T(1024)(128)(4,1)S(1)}, s32[]{:S(2)}) async-start(s8[5242880]{0:T(1024)(128)(4,1)} %bitcast.158), calls=%async_computation.1 | async-start | bytes 8388608
  604.4 8.1 %slice-start.1 = ((s8[5242880]{0:T(1024)(128)(4,1)}), s8[1048576]{0:T(1024)(128)(4,1)S(1)}, s32[]{:S(2)}) async-start(s8[5242880]{0:T(1024)(128)(4,1)} %bitcast.158), calls=%async_computation.2 | async-start | bytes 2097152
  620.9 8.1 %copy-start.9 = (bf16[640,4096]{1,0:T(8,128)(2,1)S(1)}, bf16[640,4096]{1,0:T(8,128)(2,1)}, u32[]{:S(2)}) copy-start(bf16[640,4096]{1,0:T(8,128)(2,1)} %copy-done.8) | copy-start | bytes 15728644
where the time goes:
time: 649 us; the launch traced here: 642 us
  matrix products  234 us (36%)
  blocking collectives  187 us (29%)
  local copies, waits for them, and re-layouts  119 us (18%)
  other arithmetic  80.3 us (12%)
  waiting for transfers between devices  15.8 us (2%)
    all_to_all x1, blocking collectives, shards(): lax.all_to_all(outgoing, 'bins', split_axis=2, concat_axis=1, tiled=True)  187 us
    dot_general x6, matrix products, complex_product(): jnp.einsum(form, left_real, right_imag, preferred_element_type=jnp.float32)  93.1 us
    dot_general x6, matrix products, complex_product(): jnp.einsum(form, left_real, right_real, preferred_element_type=jnp.float32)  51.5 us
    dot_general x6, matrix products, complex_product(): jnp.einsum(form, left_imag, right_imag, preferred_element_type=jnp.float32)  39.7 us
    dot_general x1, other arithmetic, migrate(): jnp.einsum('sprj,rjk->sprk', windows, band_matrix, preferred_element_type...  38.2 us
    dot_general x6, matrix products, complex_product(): jnp.einsum(form, left_imag, right_real, preferred_element_type=jnp.float32)  37.1 us
    convert_element_type x2, local copies, waits for them, and re-layouts, migrate(): return result.reshape(2, row_count, line_width).astype(jnp.bfloat16)  26.1 us
    concatenate x1, local copies, waits for them, and re-layouts, migrate(): jnp.concatenate([extended[:, :, :line_width].reshape(2, row_count, blocks...  23.6 us
  transfers between devices with their start and end apart: 1, of which 1 were waited for; matrix products, arithmetic and copies ran while one was open for 1% of the time, Pallas kernels for 0%

commit v1 on v0

--- a/solution.py
+++ b/solution.py
@@ -97,7 +97,13 @@
     compressed = compress_lines(echo_lines, range_phase)
     empty_rim = jnp.zeros((2, compressed.shape[1], 128), jnp.bfloat16)
     outgoing = migrate(compressed, empty_rim, band_start, band_weight)
-    turned = lax.all_to_all(outgoing, "bins", split_axis=2, concat_axis=1, tiled=True)
+    find_task = lambda page, group_axis, at_axis, in_dim: jnp.concatenate(
+        lax.all_to_all(
+            jnp.stack(jnp.split(page, lax.psum(1, group_axis), axis=at_axis)), group_axis, 0, 0
+        ),
+        in_dim,
+    )
+    turned = find_task(outgoing, "bins", 2, 1)
     head_lines = passed_along(turned[:, :OVLMAX], "az", -1)
     aperture = jnp.concatenate([turned, head_lines], axis=1)
     own_count = turned.shape[1]

time: 649 us -> 628 us (0.968)
  local copies, waits for them, and re-layouts: 119 us -> 96.6 us
    all_to_all x2 -> x0, local copies, waits for them, and re-layouts: 22.6 us -> none  [shards(): lax.all_to_all(outgoing, 'bins', split_axis=2, concat_axis=1, tiled=True)]
    convert_element_type x2 -> x1, local copies, waits for them, and re-layouts: 26.1 us -> 10.5 us  [migrate(): return result.reshape(2, row_count, line_width).astype(jnp.bfloat16)]
    reshape x0 -> x1, local copies, waits for them, and re-layouts: none -> 12 us  [shards(): jnp.concatenate(lax.all_to_all(jnp.stack(jnp.split(page, lax.psum(1, grou...]
where the time goes in v1:
time: 628 us; the launch traced here: 620 us
  matrix products  235 us (37%)
  blocking collectives  188 us (30%)
  local copies, waits for them, and re-layouts  96.6 us (15%)
  other arithmetic  81.5 us (13%)
  waiting for transfers between devices  15.8 us (3%)
    all_to_all x1, blocking collectives, shards(): lax.all_to_all(jnp.stack(jnp.split(page, lax.psum(1, group_axis), axis=at...  188 us
    dot_general x6, matrix products, complex_product(): jnp.einsum(form, left_real, right_imag, preferred_element_type=jnp.float32)  93.1 us
    dot_general x6, matrix products, complex_product(): jnp.einsum(form, left_real, right_real, preferred_element_type=jnp.float32)  51.5 us
    dot_general x6, matrix products, complex_product(): jnp.einsum(form, left_imag, right_imag, preferred_element_type=jnp.float32)  39.7 us
    dot_general x1, other arithmetic, migrate(): jnp.einsum('sprj,rjk->sprk', windows, band_matrix, preferred_element_type...  38.2 us
    dot_general x6, matrix products, complex_product(): jnp.einsum(form, left_imag, right_real, preferred_element_type=jnp.float32)  37.1 us
    concatenate x1, local copies, waits for them, and re-layouts, migrate(): jnp.concatenate([extended[:, :, :line_width].reshape(2, row_count, blocks...  23.7 us
    ppermute x1, waiting for transfers between devices, passed_along(): lax.ppermute(value, axis, [(source, source + steps) for source in range(f...  15.8 us
  transfers between devices with their start and end apart: 1, of which 1 were waited for; matrix products, arithmetic and copies ran while one was open for 1% of the time, Pallas kernels for 0%

profile of v1, /device:TPU:1, one launch (start us, length us, event | category | flops | bytes accessed | tf_op | source)
XLA Modules:
  0.0 620.3 jit_solution(1054975798849662732)
XLA Ops:
  0.0 3.9 slice_bitcast_fusion.7
  3.9 1.2 copy.44
  5.1 4.9 fusion.105
  10.0 4.7 fusion.99
  16.2 4.7 fusion.97
  20.9 10.6 %fusion.42 = (bf16[128,128,128]{2,1,0:T(8,128)(2,1)S(1)}, bf16[128,128,128]{2,1,0:T(8,128)(2,1)S(1)}) fusion(f32[128,128]{1,0:T(8,128)S(1)} %get-tuple-element.41, f32[128,128]{1,0:T(8,128)S(1)} %get-tuple-element.42, f32[128,128,128]{2,0,1:T(8,128)} %fusion.105, f32[128,128,128]{2,0,1:T(8,128)} %fusion.97, f32[128,128,128]{2,0,1:T(8,128)} %fusion.99, ...), kind=kOutput, calls=%fused_computation.65 | convolution fusion | flops 558088192 | bytes 37879808 | tf_op jit(solution)/shard_map/ka,pan->pkn/dot_general | solution.py:31
  31.5 4.9 fusion.101
  36.4 4.7 fusion.95
  41.1 4.7 fusion.103
  46.2 13.0 %add_convert_fusion.2 = (bf16[128,128,128]{2,1,0:T(8,128)(2,1)S(1)}, bf16[128,128,128]{2,1,0:T(8,128)(2,1)S(1)}) fusion(f32[128,128]{1,0:T(8,128)S(1)} %copy.27, f32[128,128]{1,0:T(8,128)S(1)} %copy.26, f32[128,128,128]{2,1,0:T(8,128)} %fusion.101, f32[128,128,128]{2,1,0:T(8,128)} %fusion.103, f32[128,128,128]{2,1,0:T(8,128)} %fusion.95, ...), kind=kOutput, calls=%fused_computation.46 | convolution fusion | flops 558088192 | bytes 37879808 | tf_op jit(solution)/shard_map/pkn,nm->pkm/dot_general | solution.py:34
  59.2 4.7 fusion.83
  63.9 4.9 fusion.89
  69.1 4.7 fusion.91
  73.8 12.9 %subtract_convert_fusion.1 = (bf16[128,128,128]{2,1,0:T(8,128)(2,1)}, bf16[128,128,128]{2,1,0:T(8,128)(2,1)S(1)}) fusion(f32[128,128]{1,0:T(8,128)S(1)} %get-tuple-element.43, f32[128,128]{1,0:T(8,128)S(1)} %get-tuple-element.44, f32[128,128,128]{2,1,0:T(8,128)} %fusion.89, f32[128,128,128]{2,1,0:T(8,128)} %fusion.91, f32[128,128,128]{2,1,0:T(8,128)} %fusion.83, ...), kind=kOutput, calls=%fused_computation.45 | convolution fusion | flops 558088192 | bytes 37879808 | tf_op jit(solution)/shard_map/pkm,mn->pkn/dot_general | solution.py:34
  86.7 4.9 fusion.79
  91.6 1.5 fusion.77
  93.1 10.6 %subtract_bitcast_fusion.1 = (f32[1,128,128,128]{2,3,1,0:T(8,128)}, f32[128,128,128]{1,2,0:T(8,128)}) fusion(f32[128,128,128]{2,1,0:T(8,128)} %fusion.79, bf16[128,128,128]{2,1,0:T(8,128)(2,1)S(1)} %copy-done.1), kind=kOutput, calls=%fused_computation.79 | convolution fusion | flops 539213824 | bytes 29360128 | tf_op jit(solution)/shard_map/ak,pkn->pan/dot_general | solution.py:31
  103.8 7.5 %add_bitcast_fusion.1 = (f32[1,128,128,128]{2,3,1,0:T(8,128)}, f32[128,128,128]{1,2,0:T(8,128)}) fusion(f32[128,128,128]{2,1,0:T(8,128)S(1)} %fusion.77, bf16[128,128,128]{2,1,0:T(8,128)(2,1)S(1)} %get-tuple-element.16), kind=kOutput, calls=%fused_computation.77 | convolution fusion | flops 539213824 | bytes 29360128 | tf_op jit(solution)/shard_map/ak,pkn->pan/dot_general | solution.py:34
  111.3 9.4 %copy.32 = f32[128,128,128]{0,2,1:T(8,128)} copy(f32[128,128,128]{1,2,0:T(8,128)} %get-tuple-element.24) | data formatting | bytes 16777216 | tf_op jit(solution)/shard_map/sub | solution.py:31
  120.7 9.4 %copy.33 = f32[128,128,128]{0,2,1:T(8,128)} copy(f32[128,128,128]{1,2,0:T(8,128)} %get-tuple-element.26) | data formatting | bytes 16777216 | tf_op jit(solution)/shard_map/add | solution.py:34
  130.1 6.7 %fusion.1 = bf16[2,128,16384]{1,2,0:T(8,128)(2,1)S(1)} fusion(f32[1,128,16384]{1,2,0:T(8,128)} %bitcast.152, f32[1,128,16384]{1,2,0:T(8,128)} %bitcast.151), kind=kLoop, calls=%fused_computation.3 | loop fusion | flops 12582912 | bytes 25165824 | tf_op jit(solution)/shard_map/convert_element_type | solution.py:68
  136.7 3.7 pad_slice_fusion
  140.4 13.5 %copy.34 = bf16[2,128,128,128]{2,3,1,0:T(8,128)(2,1)} copy(bf16[2,128,128,128]{1,3,2,0:T(8,128)(2,1)} %bitcast.154) | data formatting | bytes 16777216 | tf_op jit(solution)/shard_map/reshape | solution.py:78
  153.9 7.1 %fusion = bf16[2,128,128,128]{2,3,1,0:T(8,128)(2,1)S(1)} fusion(f32[1,128,128,128]{2,3,1,0:T(8,128)} %get-tuple-element.25, f32[1,128,128,128]{2,3,1,0:T(8,128)} %get-tuple-element.23), kind=kLoop, calls=%fused_computation.1 | loop fusion | flops 12582912 | bytes 25165824 | tf_op jit(solution)/shard_map/convert_element_type | solution.py:68
  162.2 6.5 %pad_maximum_fusion = bf16[2,128,128,256]{2,3,1,0:T(8,128)(2,1)} fusion(bf16[2,128,128,128]{2,3,1,0:T(8,128)(2,1)S(1)} %copy-done.2, bf16[2,128,128,128]{2,3,1,0:T(8,128)(2,1)S(1)} %fusion), kind=kLoop, calls=%fused_computation.4 | loop fusion | flops 33554432 | bytes 33554432 | tf_op jit(solution)/shard_map/concatenate | solution.py:75
  168.7 23.7 %copy.35 = bf16[2,128,128,256]{3,1,0,2:T(8,128)(2,1)} copy(bf16[2,128,128,256]{2,3,1,0:T(8,128)(2,1)} %pad_maximum_fusion) | data formatting | bytes 33554432 | tf_op jit(solution)/shard_map/concatenate | solution.py:75
  192.5 1.4 slice_reduce_fusion.7
  193.9 38.2 %fusion.232 = bf16[128,256,128,1]{1,2,3,0:T(8,128)(2,1)} fusion(s32[128,128]{1,0:T(8,128)S(1)} %get-tuple-element.38, s32[128,128]{1,0:T(8,128)S(1)} %get-tuple-element.34, s32[128,128]{1,0:T(8,128)S(1)} %get-tuple-element.35, s32[128,128]{1,0:T(8,128)S(1)} %get-tuple-element.36, s32[128,128]{1,0:T(8,128)S(1)} %get-tuple-element.37, ...), kind=kLoop, calls=%fused_computation.32.clone.clone.clone.clone.1 | loop fusion | flops 134217728 | bytes 9175040 | tf_op jit(solution)/shard_map/sprj,rjk->sprk/dot_general | solution.py:91
  232.1 13.1 %convert_bitcast_fusion = bf16[2,128,128,128]{1,3,0,2:T(8,128)(2,1)} fusion(bf16[2,128,128,256]{3,1,0,2:T(8,128)(2,1)} %copy.35, bf16[128,256,128,1]{1,2,3,0:T(8,128)(2,1)} %fusion.232), kind=kOutput, calls=%fused_computation.43 | convolution fusion | flops 2151677952 | bytes 33554432 | tf_op jit(solution)/shard_map/sprj,rjk->sprk/dot_general | solution.py:91
  245.2 10.5 %copy.36 = bf16[2,128,128,128]{1,3,2,0:T(8,128)(2,1)} copy(bf16[2,128,128,128]{1,3,0,2:T(8,128)(2,1)} %convert_bitcast_fusion) | data formatting | bytes 16777216 | tf_op jit(solution)/shard_map/convert_element_type | solution.py:92
  255.7 3.7 slice_bitcast_fusion.11
  260.5 187.5 %all_to_all.5 = bf16[4,2,128,4096]{2,3,1,0:T(8,128)(2,1)} all-to-all(bf16[4,2,128,4096]{2,3,1,0:T(8,128)(2,1)S(1)} %pad_maximum_fusion.1), channel_id=1, replica_groups=mesh['scene'=2,'bins'=4,'az'=4] {'bins'}, dimensions={0} | all-to-all | bytes 16777216 | tf_op jit(solution)/shard_map/all_to_all | solution.py:101
  448.1 12.0 %copy.37 = bf16[2,4,128,4096]{3,2,1,0:T(8,128)(2,1)} copy(bf16[2,4,128,4096]{2,3,0,1:T(8,128)(2,1)} %bitcast.155) | data formatting | bytes 16777216 | tf_op jit(solution)/shard_map/reshape | solution.py:100
  460.1 1.7 slice.58
  461.8 3.7 collective-permute-start
  465.5 6.5 %cosine_convert_fusion.2.clone.5 = bf16[640,640]{1,0:T(8,128)(2,1)S(1)} fusion(), kind=kLoop, calls=%fused_computation.90.clone.clone.clone.clone.2 | loop fusion | flops 4096000 | bytes 819200 | tf_op jit(solution)/shard_map/convert_element_type | solution.py:25
  472.1 2.3 compare_or_fusion
  474.4 15.8 %collective-permute-done = bf16[2,128,4096]{2,1,0:T(8,128)(2,1)S(1)} collective-permute-done((bf16[2,128,4096]{2,1,0:T(8,128)(2,1)S(1)}, bf16[2,128,4096]{2,1,0:T(8,128)(2,1)S(1)}, u32[]{:S(2)}, u32[]{:S(2)}) %collective-permute-start) | collective-permute-done | bytes 2097184 | tf_op jit(solution)/shard_map/ppermute | solution.py:13
  490.3 7.9 %maximum_select_fusion = bf16[2,640,4096]{2,1,0:T(8,128)(2,1)S(1)} fusion(bf16[2,128,4096]{2,1,0:T(8,128)(2,1)S(1)} %collective-permute-done, bf16[2,512,4096]{2,1,0:T(8,128)(2,1)} %bitcast.146, pred[640,4096]{1,0:T(8,128)(4,1)S(1)} %compare_or_fusion), kind=kLoop, calls=%fused_computation.23 | loop fusion | flops 26214400 | bytes 23592960 | tf_op jit(solution)/shard_map/jit(_where)/select_n | solution.py:113
  498.2 12.6 %fusion.40 = f32[640,4096]{1,0:T(8,128)} fusion(bf16[2,640,4096]{2,1,0:T(8,128)(2,1)S(1)} %maximum_select_fusion), kind=kOutput, calls=%fused_computation.63 | convolution fusion | flops 3359539200 | bytes 15728640 | tf_op jit(solution)/shard_map/fp,pr->fr/dot_general | solution.py:33
  510.8 12.9 %fusion.39 = f32[640,4096]{1,0:T(8,128)} fusion(bf16[2,640,4096]{2,1,0:T(8,128)(2,1)S(1)} %maximum_select_fusion), kind=kOutput, calls=%fused_computation.62 | convolution fusion | flops 3359539200 | bytes 15728640 | tf_op jit(solution)/shard_map/fp,pr->fr/dot_general | solution.py:36
  523.8 12.9 %convolution_subtract_fusion = f32[640,4096]{1,0:T(8,128)S(1)} fusion(f32[640,4096]{1,0:T(8,128)} %fusion.40, bf16[2,640,4096]{2,1,0:T(8,128)(2,1)S(1)} %maximum_select_fusion), kind=kOutput, calls=%fused_computation.59 | convolution fusion | flops 3362160640 | bytes 26214400 | tf_op jit(solution)/shard_map/fp,pr->fr/dot_general | solution.py:31
  536.6 46.4 %subtract_convert_fusion = (bf16[640,4096]{1,0:T(8,128)(2,1)S(1)}, bf16[640,4096]{1,0:T(8,128)(2,1)}) fusion(f32[640,4096]{1,0:T(8,128)S(1)} %convolution_subtract_fusion, f32[640]{0:T(1024)S(1)} %fusion.111, f32[4096]{0:T(1024)S(1)} %broadcast_multiply_fusion, f32[640,4096]{1,0:T(8,128)} %fusion.39, bf16[2,640,4096]{2,1,0:T(8,128)(2,1)S(1)} %maximum_select_fusion, ...), kind=kOutput, calls=%fused_computation.25 | convolution fusion | flops 3386900480 | bytes 37539840 | tf_op jit(solution)/shard_map/fp,pr->fr/dot_general | solution.py:34
  583.1 8.0 %fusion.63 = f32[512,4096]{1,0:T(8,128)S(1)} fusion(bf16[640,4096]{1,0:T(8,128)(2,1)S(1)} %get-tuple-element.21), kind=kOutput, calls=%fused_computation.104 | convolution fusion | flops 2687631360 | bytes 13631488 | tf_op jit(solution)/shard_map/qf,fr->qr/dot_general | solution.py:31
  591.2 8.4 %fusion.62 = f32[512,4096]{1,0:T(8,128)S(1)} fusion(bf16[640,4096]{1,0:T(8,128)(2,1)S(1)} %bitcast.165), kind=kOutput, calls=%fused_computation.103 | convolution fusion | flops 2687631360 | bytes 13631488 | tf_op jit(solution)/shard_map/qf,fr->qr/dot_general | solution.py:34
  599.6 8.1 %subtract_bitcast_fusion = f32[1,1,512,4096]{3,2,1,0:T(8,128)S(1)} fusion(f32[512,4096]{1,0:T(8,128)S(1)} %fusion.63, bf16[640,4096]{1,0:T(8,128)(2,1)S(1)} %bitcast.165), kind=kOutput, calls=%fused_computation.42 | convolution fusion | flops 2689728512 | bytes 22020096 | tf_op jit(solution)/shard_map/qf,fr->qr/dot_general | solution.py:33
  607.7 8.3 %add_bitcast_fusion = f32[1,1,512,4096]{3,2,1,0:T(8,128)S(1)} fusion(f32[512,4096]{1,0:T(8,128)S(1)} %fusion.62, bf16[640,4096]{1,0:T(8,128)(2,1)S(1)} %copy-done.9), kind=kOutput, calls=%fused_computation.41 | convolution fusion | flops 2689728512 | bytes 22020096 | tf_op jit(solution)/shard_map/qf,fr->qr/dot_general | solution.py:36
  616.0 4.1 fusion.2
  (39 shorter events, 4.6 us)
Async XLA Ops:
  31.5 9.6 %copy-start = (bf16[128,128,128]{2,1,0:T(8,128)(2,1)}, bf16[128,128,128]{2,1,0:T(8,128)(2,1)S(1)}, u32[]{:S(2)}) copy-start(bf16[128,128,128]{2,1,0:T(8,128)(2,1)S(1)} %get-tuple-element.20) | copy-start | bytes 12582916
  41.1 4.7 copy-start.4
  86.7 4.9 copy-start.1
  153.9 8.2 %copy-start.2 = (bf16[2,128,128,128]{2,3,1,0:T(8,128)(2,1)S(1)}, bf16[2,128,128,128]{2,3,1,0:T(8,128)(2,1)}, u32[]{:S(2)}) copy-start(bf16[2,128,128,128]{2,3,1,0:T(8,128)(2,1)} %copy.34) | copy-start | bytes 25165828
  168.7 23.7 %copy-start.5 = (s32[16384]{0:T(1024)S(1)}, s32[16384]{0:T(1024)}, u32[]{:S(2)}) copy-start(s32[16384]{0:T(1024)} %param.8) | copy-start | bytes 196612
  168.7 23.8 %copy-start.3 = (bf16[8,16384]{1,0:T(8,128)(2,1)S(1)}, bf16[8,16384]{1,0:T(8,128)(2,1)}, u32[]{:S(2)}) copy-start(bf16[8,16384]{1,0:T(8,128)(2,1)} %param.9) | copy-start | bytes 786436
  448.1 24.0 %copy-start.7 = (f32[4096]{0:T(1024)S(1)}, f32[4096]{0:T(1024)}, u32[]{:S(2)}) copy-start(f32[4096]{0:T(1024)} %param.11) | copy-start | bytes 49156
  448.1 24.0 %copy-start.6 = (s32[4096]{0:T(1024)S(1)}, s32[4096]{0:T(1024)}, u32[]{:S(2)}) copy-start(s32[4096]{0:T(1024)} %param.10) | copy-start | bytes 49156
  461.8 28.5 %collective-permute-start = (bf16[2,128,4096]{2,1,0:T(8,128)(2,1)S(1)}, bf16[2,128,4096]{2,1,0:T(8,128)(2,1)S(1)}, u32[]{:S(2)}, u32[]{:S(2)}) collective-permute-start(bf16[2,128,4096]{2,1,0:T(8,128)(2,1)S(1)} %slice.58), channel_id=1, source_target_pairs={{1,0},{2,1},{3,2},{5,4},{6,5},{7,6},{9,8},{10,9},{11,10},{13,12},{... | collective-permute-start | bytes 6291464 | tf_op jit(solution)/shard_map/ppermute | solution.py:13
  583.1 8.1 %copy-start.8 = (bf16[640,4096]{1,0:T(8,128)(2,1)}, bf16[640,4096]{1,0:T(8,128)(2,1)S(1)}, u32[]{:S(2)}) copy-start(bf16[640,4096]{1,0:T(8,128)(2,1)S(1)} %get-tuple-element.21) | copy-start | bytes 15728644
  583.1 8.1 %slice-start = ((s8[5242880]{0:T(1024)(128)(4,1)}), s8[4194304]{0:T(1024)(128)(4,1)S(1)}, s32[]{:S(2)}) async-start(s8[5242880]{0:T(1024)(128)(4,1)} %bitcast.164), calls=%async_computation.1 | async-start | bytes 8388608
  583.1 8.1 %slice-start.1 = ((s8[5242880]{0:T(1024)(128)(4,1)}), s8[1048576]{0:T(1024)(128)(4,1)S(1)}, s32[]{:S(2)}) async-start(s8[5242880]{0:T(1024)(128)(4,1)} %bitcast.164), calls=%async_computation.2 | async-start | bytes 2097152
  599.6 8.1 %copy-start.9 = (bf16[640,4096]{1,0:T(8,128)(2,1)S(1)}, bf16[640,4096]{1,0:T(8,128)(2,1)}, u32[]{:S(2)}) copy-start(bf16[640,4096]{1,0:T(8,128)(2,1)} %copy-done.8) | copy-start | bytes 15728644
